TPU v7x, 32 devices: a whole 2x2x4 slice. The times are simulated.
32 devices in a mesh: section: 2 (over x), dp: 4 (over z), tensor: 4 (over y, core).
Axes of the slice: x: 2, y: 2, z: 4, core: 2. Of those that a mesh axis runs over, the one named last changes fastest.
Arguments:
- layer_in: bfloat16 [2, 32, 8192], P('section', 'dp'), may hold values from -6 to 6
- ln_gain: float32 [2, 8192], P('section'), may hold values from 0.25 to 1.75
- ln_bias: float32 [2, 8192], P('section'), may hold values from -2 to 2
- w_up: bfloat16 [2, 8192, 32768], P('section', 'tensor', 'dp'), may hold values from -0.0625 to 0.0625
- b_up: float32 [2, 32768], P('section', 'dp'), may hold values from -3 to 3
- w_down: bfloat16 [2, 32768, 8192], P('section', 'dp', 'tensor'), may hold values from -0.03125 to 0.03125
- b_down: float32 [2, 8192], P('section', 'tensor'), may hold values from -3 to 3
Outputs:
- handed: bfloat16 [2, 32, 8192], P('section', 'dp')
All inputs are finite; a program needn't handle non-finite values.
Results may differ from a plain program's by a relative error of at most 0.0042.
Values may be sent and summed in bfloat16 or wider, within the bound.
A program may use at most 192 MiB of HBM per device.

v0:
```python
import jax
import jax.numpy as jnp
from jax import lax
from jax.sharding import PartitionSpec as P


def shifted(value, axis, steps):
    count = lax.axis_size(axis)
    pairs = [(source, (source + steps) % count) for source in range(count)]
    return lax.ppermute(value, axis, pairs)


def shards(layer_in, ln_gain, ln_bias, w_up, b_up, w_down, b_down):
    rows = layer_in[0]
    up_local = w_up[0]
    down_local = w_down[0]
    part_width = up_local.shape[0]
    offset = lax.axis_index("tensor") * part_width
    values = rows.astype(jnp.float32)
    center = jnp.mean(values, axis=1, keepdims=True)
    spread = jnp.mean(jnp.square(values - center), axis=1, keepdims=True)
    scaled = (values - center) * lax.rsqrt(spread + 1e-05)
    own_scaled = lax.dynamic_slice_in_dim(scaled, offset, part_width, 1)
    own_gain = lax.dynamic_slice_in_dim(ln_gain[0], offset, part_width, 0)
    own_shift = lax.dynamic_slice_in_dim(ln_bias[0], offset, part_width, 0)
    normed = (own_scaled * own_gain + own_shift).astype(jnp.bfloat16)
    partial_up = jnp.dot(
        lax.all_gather(normed, "dp", axis=0, tiled=True),
        up_local,
        preferred_element_type=jnp.float32,
    )
    share = lax.psum_scatter(partial_up, "tensor", scatter_dimension=0, tiled=True)
    share_hidden = jax.nn.gelu(share + b_up[0], approximate=True).astype(jnp.bfloat16)
    hidden = lax.all_gather(share_hidden, "tensor", axis=0, tiled=True)
    reduced = lax.psum_scatter(
        jnp.dot(hidden, down_local, preferred_element_type=jnp.float32),
        "dp",
        scatter_dimension=0,
        tiled=True,
    )
    own_values = lax.dynamic_slice_in_dim(values, offset, part_width, 1)
    out_part = (reduced + b_down[0] + own_values).astype(jnp.bfloat16)
    full_rows = lax.all_gather(out_part, "tensor", axis=1, tiled=True)
    arrived = shifted(full_rows, "section", 1)
    return arrived[None]


def solution(mesh):
    return jax.shard_map(
        shards,
        mesh=mesh,
        in_specs=(
            P("section", "dp", None),
            P("section", None),
            P("section", None),
            P("section", "tensor", "dp"),
            P("section", "dp"),
            P("section", "dp", "tensor"),
            P("section", "tensor"),
        ),
        out_specs=P("section", "dp", None),
        check_vma=False,
    )
```

profile of v0, /device:TPU:0, one launch (start us, length us, event | category | flops | bytes accessed | tf_op | source)
XLA Modules:
  0.0 127.4 jit_solution(2634127204252372337)
XLA Ops:
  6.5 0.0 copy-start.1
  6.5 0.0 reduce-scatter.3.cloned.1.call-start
  6.5 1.1 convert_reduce_fusion
  7.6 1.2 multiply_reduce_fusion
  8.8 0.7 constant_dynamic-slice_fusion
  9.5 0.1 fusion.14
  9.6 15.1 %all_gather.9 = bf16[32,2048]{1,0:T(8,128)(2,1)S(1)} all-gather(bf16[8,2048]{1,0:T(8,128)(2,1)S(1)} %fusion.14), channel_id=1, replica_groups=mesh['section'=2,'dp'=4,'tensor'=4] {'dp'}, dimensions={0}, use_global_device_ids=true | all-gather | bytes 163840 | tf_op jit(solution)/shard_map/all_gather | solution.py:28
  24.7 14.6 %fusion.2 = f32[32,8192]{1,0:T(8,128)} fusion(bf16[32,2048]{1,0:T(8,128)(2,1)S(1)} %all_gather.9, bf16[1,2048,8192]{2,1,0:T(8,128)(2,1)} %param.10), kind=kOutput, calls=%fused_computation.2 | convolution fusion | flops 1073741824 | bytes 34734080 | tf_op jit(solution)/shard_map/dot_general | solution.py:27
  39.2 0.0 reduce-scatter.3.cloned.1.call-update
  39.3 0.0 reduce-scatter.5.cloned.1.call-start
  39.3 26.3 %reduce-scatter.3.cloned.1.call-done = f32[8,8192]{1,0:T(8,128)} async-done(((f32[32,8192]{1,0:T(8,128)}), f32[8,8192]{1,0:T(8,128)}) %reduce-scatter.3.cloned.1.call-update) | async-done | bytes 262160 | tf_op jit(solution)/shard_map/reduce_scatter | solution.py:32
  65.6 0.0 copy-done.1
  65.6 1.0 fusion.11
  66.7 6.8 %all_gather.10 = bf16[32,8192]{1,0:T(8,128)(2,1)S(1)} all-gather(bf16[8,8192]{1,0:T(8,128)(2,1)S(1)} %fusion.11), channel_id=1, replica_groups=mesh['section'=2,'dp'=4,'tensor'=4] {'tensor'}, dimensions={0}, use_global_device_ids=true | all-gather | bytes 655360 | tf_op jit(solution)/shard_map/all_gather | solution.py:34
  73.5 14.2 %fusion = f32[32,2048]{1,0:T(8,128)} fusion(bf16[32,8192]{1,0:T(8,128)(2,1)S(1)} %all_gather.10, bf16[1,8192,2048]{2,1,0:T(8,128)(2,1)} %param.12), kind=kOutput, calls=%fused_computation | convolution fusion | flops 1073741824 | bytes 34340864 | tf_op jit(solution)/shard_map/dot_general | solution.py:36
  87.7 0.0 reduce-scatter.5.cloned.1.call-update
  87.7 0.0 copy-done
  87.8 20.1 %reduce-scatter.5.cloned.1.call-done = f32[8,2048]{1,0:T(8,128)} async-done(((f32[32,2048]{1,0:T(8,128)}), f32[8,2048]{1,0:T(8,128)}) %reduce-scatter.5.cloned.1.call-update) | async-done | bytes 65552 | tf_op jit(solution)/shard_map/reduce_scatter | solution.py:35
  107.9 0.0 copy-done.2
  107.9 0.9 fusion.15
  108.8 5.4 %all_gather.11 = bf16[8,8192]{1,0:T(8,128)(2,1)S(1)} all-gather(bf16[8,2048]{1,0:T(8,128)(2,1)S(1)} %fusion.15), channel_id=1, replica_groups=mesh['section'=2,'dp'=4,'tensor'=4] {'tensor'}, dimensions={1}, use_global_device_ids=true | all-gather | bytes 163840 | tf_op jit(solution)/shard_map/all_gather | solution.py:43
  114.2 1.5 %collective-permute-start = (bf16[8,8192]{1,0:T(8,128)(2,1)S(1)}, bf16[8,8192]{1,0:T(8,128)(2,1)S(1)}, u32[]{:S(2)}, u32[]{:S(2)}) collective-permute-start(bf16[8,8192]{1,0:T(8,128)(2,1)S(1)} %all_gather.11), channel_id=1, source_target_pairs={{0,16},{16,0},{1,17},{17,1},{2,18},{18,2},{3,19},{19,3},{4,20},{20... | collective-permute-start | bytes 393224 | tf_op jit(solution)/shard_map/ppermute | solution.py:10
  115.7 4.3 %collective-permute-done = bf16[8,8192]{1,0:T(8,128)(2,1)S(1)} collective-permute-done((bf16[8,8192]{1,0:T(8,128)(2,1)S(1)}, bf16[8,8192]{1,0:T(8,128)(2,1)S(1)}, u32[]{:S(2)}, u32[]{:S(2)}) %collective-permute-start) | collective-permute-done | bytes 131104 | tf_op jit(solution)/shard_map/ppermute | solution.py:10
  119.9 0.7 copy.9
  (5 shorter events, 0.0 us)
Async XLA Ops:
  6.5 59.1 %copy-start.1 = (f32[1,8192]{1,0:T(1,128)S(1)}, f32[1,8192]{1,0:T(1,128)}, u32[]{:S(2)}) copy-start(f32[1,8192]{1,0:T(1,128)} %param.11) | copy-start | bytes 98308
  6.5 59.1 %reduce-scatter.3.cloned.1.call-start = ((), (), s32[]{:S(2)}) async-start(), calls=%async_computation.2 | async-start | bytes 1310720 | tf_op jit(solution)/shard_map/reduce_scatter | solution.py:32
  24.7 63.1 %copy-start = (bf16[1,8,8192]{2,1,0:T(8,128)(2,1)S(1)}, bf16[1,8,8192]{2,1,0:T(8,128)(2,1)}, u32[]{:S(2)}) copy-start(bf16[1,8,8192]{2,1,0:T(8,128)(2,1)} %param.7) | copy-start | bytes 393220
  24.7 83.2 %copy-start.2 = (f32[1,2048]{1,0:T(1,128)S(1)}, f32[1,2048]{1,0:T(1,128)}, u32[]{:S(2)}) copy-start(f32[1,2048]{1,0:T(1,128)} %param.13) | copy-start | bytes 24580
  39.3 68.7 %reduce-scatter.5.cloned.1.call-start = ((), (), s32[]{:S(2)}) async-start(), calls=%async_computation.3 | async-start | bytes 327680 | tf_op jit(solution)/shard_map/reduce_scatter | solution.py:35
  114.2 5.7 %collective-permute-start = (bf16[8,8192]{1,0:T(8,128)(2,1)S(1)}, bf16[8,8192]{1,0:T(8,128)(2,1)S(1)}, u32[]{:S(2)}, u32[]{:S(2)}) collective-permute-start(bf16[8,8192]{1,0:T(8,128)(2,1)S(1)} %all_gather.11), channel_id=1, source_target_pairs={{0,16},{16,0},{1,17},{17,1},{2,18},{18,2},{3,19},{19,3},{4,20},{20... | collective-permute-start | bytes 393224 | tf_op jit(solution)/shard_map/ppermute | solution.py:10
Sparse Core Ops, SparseCore 0:
  39.4 26.2 reduce-scatter.2
  87.9 20.0 reduce-scatter.4
where the time goes:
time: 128 us; the launch traced here: 127 us
  waiting for transfers between devices  50.8 us (40%)
  matrix products  28.8 us (22%)
  blocking collectives  27.3 us (21%)
  between operations  13.4 us (10%)
  other arithmetic  4.26 us (3%)
  starting transfers between devices  1.51 us (1%)
  local copies, waits for them, and re-layouts  1.39 us (1%)
    reduce_scatter x1, waiting for transfers between devices, shards(): lax.psum_scatter(partial_up, 'tensor', scatter_dimension=0, tiled=True)  26.3 us
    reduce_scatter x1, waiting for transfers between devices, shards(): lax.psum_scatter(jnp.dot(hidden, down_local, preferred_element_type=jnp.f...  20.1 us
    all_gather x1, blocking collectives, shards(): lax.all_gather(normed, 'dp', axis=0, tiled=True)  15.1 us
    dot_general x1, matrix products, shards(): jnp.dot(lax.all_gather(normed, 'dp', axis=0, tiled=True), up_local, prefe...  14.6 us
    dot_general x1, matrix products, shards(): jnp.dot(hidden, down_local, preferred_element_type=jnp.float32)  14.2 us
    all_gather x1, blocking collectives, shards(): hidden = lax.all_gather(share_hidden, 'tensor', axis=0, tiled=True)  6.79 us
    all_gather x1, blocking collectives, shards(): full_rows = lax.all_gather(out_part, 'tensor', axis=1, tiled=True)  5.43 us
    ppermute x1, waiting for transfers between devices, shifted(): return lax.ppermute(value, axis, pairs)  4.28 us
  transfers between devices with their start and end apart: 3, of which 3 were waited for; matrix products, arithmetic and copies ran while one was open for 0% of the time, Pallas kernels for 0%

commit v1 on v0

v1 whole, which is shorter than its diff:
```python
import functools

import jax
import jax.numpy as jnp
from jax import lax
from jax.experimental import pallas as pl
from jax.experimental.pallas import tpu as pltpu
from jax.sharding import PartitionSpec as P

MESH = pl.DeviceIdType.MESH
BF = jnp.bfloat16
F32 = jnp.float32
LAG_ACROSS = 3
LAG_GELU = 9
LAG_DOWN = 12


def gelu(v):
    return 0.5 * v * (1.0 + jnp.tanh(0.7978845608028654 * (v + 0.044715 * (v * v * v))))


def kernel(
    sizes,
    x_hbm, gain_hbm, shift_hbm, up_hbm, bup_hbm, down_hbm, bdown_hbm,
    out_hbm,
    x_v, gain_v, shift_v, bup_v, bdown_v,
    up_v, down_v,
    norm_s, norm_r, lhs_v,
    resid_s, resid_r,
    pair_s, pair_r, keep_v,
    across_s, across_r,
    hid_v, acc_v,
    part_s, part_r, fin_v,
    in_sem, up_sem, down_sem,
    norm_ss, norm_rs, resid_ss, resid_rs,
    pair_ss, pair_rs, across_ss, across_rs, hid_ss, hid_rs,
    part_ss, part_rs, fin_ss, fin_rs, own_sem,
):
    n_sec, n_dp, n_t, chunks, slots, rows, width, cw = sizes
    outer = n_t // 2
    half = rows * n_dp // 2
    s = lax.axis_index("section")
    d = lax.axis_index("dp")
    t = lax.axis_index("tensor")
    core = lax.rem(t, 2)
    partner = t + 1 - 2 * core
    offset = pl.multiple_of(t * width, width)
    nxt = lax.rem(s + 1, n_sec)
    prv = lax.rem(s + n_sec - 1, n_sec)

    barrier = pltpu.get_barrier_semaphore()
    for k in range(1, n_dp):
        pl.semaphore_signal(barrier, inc=1, device_id=(s, lax.rem(d + k, n_dp), t), device_id_type=MESH)
    for k in range(1, n_t):
        pl.semaphore_signal(barrier, inc=1, device_id=(s, d, lax.rem(t + k, n_t)), device_id_type=MESH)
    for k in range(n_dp):
        pl.semaphore_signal(barrier, inc=1, device_id=(prv, lax.rem(d + k, n_dp), t), device_id_type=MESH)

    small = [
        pltpu.make_async_copy(x_hbm.at[0], x_v, in_sem.at[0]),
        pltpu.make_async_copy(gain_hbm.at[:, pl.ds(offset, width)], gain_v, in_sem.at[1]),
        pltpu.make_async_copy(shift_hbm.at[:, pl.ds(offset, width)], shift_v, in_sem.at[2]),
        pltpu.make_async_copy(bdown_hbm, bdown_v, in_sem.at[3]),
        pltpu.make_async_copy(bup_hbm, bup_v, in_sem.at[4]),
    ]
    for copy in small:
        copy.start()

    def up_copy(c):
        columns = pl.ds(pl.multiple_of(c * cw, cw), cw)
        return pltpu.make_async_copy(up_hbm.at[0, :, columns], up_v.at[c], up_sem.at[c])

    def down_copy(c):
        lines = pl.ds(pl.multiple_of(c * cw, cw), cw)
        slot = lax.rem(c, slots)
        return pltpu.make_async_copy(down_hbm.at[0, lines, :], down_v.at[slot], down_sem.at[slot])

    def run(count, body):
        def step(i, carry):
            body(i)
            return carry
        lax.fori_loop(0, count, step, 0)

    run(chunks, lambda c: up_copy(c).start())
    run(slots, lambda c: down_copy(c).start())

    for copy in small[:4]:
        copy.wait()
    values = x_v[...].astype(F32)
    center = jnp.mean(values, axis=1, keepdims=True)
    spread = jnp.mean(jnp.square(values - center), axis=1, keepdims=True)
    own = x_v[:, pl.ds(offset, width)].astype(F32)
    normed = (own - center) * lax.rsqrt(spread + 1e-05) * gain_v[...] + shift_v[...]
    norm_s[...] = normed.astype(BF)
    resid_s[...] = own + bdown_v[...]
    pl.semaphore_wait(barrier, 2 * n_dp + n_t - 2)

    def norm_copy(k):
        return pltpu.make_async_remote_copy(
            norm_s, norm_r.at[d], norm_ss.at[k - 1], norm_rs.at[k - 1],
            device_id=(s, lax.rem(d + k, n_dp), t), device_id_type=MESH)

    for k in range(1, n_dp):
        norm_copy(k).start()
    resid_copy = pltpu.make_async_remote_copy(
        resid_s, resid_r, resid_ss, resid_rs, device_id=(nxt, d, t), device_id_type=MESH)
    resid_copy.start()
    norm_own = pltpu.make_async_copy(norm_s, norm_r.at[d], own_sem)
    norm_own.start()
    small[4].wait()
    acc_v[...] = jnp.zeros_like(acc_v)
    norm_own.wait()
    for k in range(1, n_dp):
        norm_copy(k).wait_recv()
    lhs_v[...] = norm_r[...].astype(F32).reshape(n_dp * rows, width).astype(BF)

    def pair_copy(c):
        return pltpu.make_async_remote_copy(
            pair_s.at[c], pair_r.at[c], pair_ss.at[c], pair_rs.at[c],
            device_id=(s, d, partner), device_id_type=MESH)

    def across_copy(c, k):
        return pltpu.make_async_remote_copy(
            across_s.at[c], across_r.at[k - 1, c], across_ss.at[k - 1, c], across_rs.at[k - 1, c],
            device_id=(s, d, lax.rem(t + 2 * k, n_t)), device_id_type=MESH)

    def hid_copy(c):
        return pltpu.make_async_remote_copy(
            hid_v.at[c, core], hid_v.at[c, core], hid_ss.at[c], hid_rs.at[c],
            device_id=(s, d, partner), device_id_type=MESH)

    def up_stage(c):
        up_copy(c).wait()
        pre = jnp.dot(lhs_v[...], up_v[c], preferred_element_type=F32)
        first = core == 0
        pair_s[c] = jnp.where(first, pre[half:], pre[:half]).astype(BF)
        pair_copy(c).start()
        keep_v[c] = jnp.where(first, pre[:half], pre[half:])

    def across_stage(c):
        pair_copy(c).wait_recv()
        both = keep_v[c] + pair_r[c].astype(F32)
        across_s[c] = both.astype(BF)
        for k in range(1, outer):
            across_copy(c, k).start()
        keep_v[c] = both

    def gelu_stage(c):
        total = keep_v[c]
        for k in range(1, outer):
            across_copy(c, k).wait_recv()
            total = total + across_r[k - 1, c].astype(F32)
        total = total + bup_v[:, pl.ds(pl.multiple_of(c * cw, cw), cw)]
        hid_v[c, core] = gelu(total).astype(BF)
        hid_copy(c).start()

    def down_stage(c):
        other = pltpu.make_async_remote_copy(
            hid_v.at[c, 1 - core], hid_v.at[c, 1 - core], hid_ss.at[c], hid_rs.at[c],
            device_id=(s, d, partner), device_id_type=MESH)
        other.wait_recv()
        down_copy(c).wait()
        acc_v[...] += jnp.dot(
            hid_v[c].reshape(2 * half, cw), down_v[lax.rem(c, slots)], preferred_element_type=F32)
        if slots < chunks:
            @pl.when(c + slots < chunks)
            def _():
                down_copy(c + slots).start()

    stages = ((0, up_stage), (LAG_ACROSS, across_stage), (LAG_GELU, gelu_stage), (LAG_DOWN, down_stage))

    def tick(i):
        for lag, stage in stages:
            @pl.when((i >= lag) & (i < lag + chunks))
            def _():
                stage(i - lag)

    run(chunks + LAG_DOWN, tick)

    part_s[...] = acc_v[...].reshape(n_dp, rows, width).astype(BF)

    def part_copy(k):
        target = lax.rem(d + k, n_dp)
        return pltpu.make_async_remote_copy(
            part_s.at[target], part_r.at[k], part_ss.at[k], part_rs.at[k],
            device_id=(nxt, target, t), device_id_type=MESH)

    for k in range(n_dp):
        part_copy(k).start()
    resid_copy.wait_recv()
    total = resid_r[...]
    for k in range(n_dp):
        part_copy(k).wait_recv()
        total = total + part_r[k].astype(F32)
    fin_v[...] = total.astype(BF)

    def fin_copy(k):
        place = out_hbm.at[0, :, pl.ds(offset, width)]
        return pltpu.make_async_remote_copy(
            fin_v, place, fin_ss.at[k - 1], fin_rs.at[k - 1],
            device_id=(s, d, lax.rem(t + k, n_t)), device_id_type=MESH)

    for k in range(1, n_t):
        fin_copy(k).start()
    fin_own = pltpu.make_async_copy(fin_v, out_hbm.at[0, :, pl.ds(offset, width)], own_sem)
    fin_own.start()

    for k in range(1, n_dp):
        norm_copy(k).wait_send()
    resid_copy.wait_send()

    def drain(c):
        pair_copy(c).wait_send()
        for k in range(1, outer):
            across_copy(c, k).wait_send()
        hid_copy(c).wait_send()

    run(chunks, drain)
    for k in range(n_dp):
        part_copy(k).wait_send()
    fin_own.wait()
    for k in range(1, n_t):
        fin_copy(k).wait()


def shards(n_sec, n_dp, n_t, layer_in, ln_gain, ln_bias, w_up, b_up, w_down, b_down):
    rows = layer_in.shape[1]
    width, units = w_up.shape[1], w_up.shape[2]
    cw = 512 if units % 512 == 0 else units
    chunks = units // cw
    slots = min(chunks, 12)
    tokens = rows * n_dp
    half = tokens // 2
    outer = n_t // 2
    peers = max(outer - 1, 1)
    sizes = (n_sec, n_dp, n_t, chunks, slots, rows, width, cw)
    dma = pltpu.SemaphoreType.DMA
    scratch = [
        pltpu.VMEM((rows, layer_in.shape[2]), BF),
        pltpu.VMEM((1, width), F32),
        pltpu.VMEM((1, width), F32),
        pltpu.VMEM((1, units), F32),
        pltpu.VMEM((1, width), F32),
        pltpu.VMEM((chunks, width, cw), BF),
        pltpu.VMEM((slots, cw, width), BF),
        pltpu.VMEM((rows, width), BF),
        pltpu.VMEM((n_dp, rows, width), BF),
        pltpu.VMEM((tokens, width), BF),
        pltpu.VMEM((rows, width), F32),
        pltpu.VMEM((rows, width), F32),
        pltpu.VMEM((chunks, half, cw), BF),
        pltpu.VMEM((chunks, half, cw), BF),
        pltpu.VMEM((chunks, half, cw), F32),
        pltpu.VMEM((chunks, half, cw), BF),
        pltpu.VMEM((peers, chunks, half, cw), BF),
        pltpu.VMEM((chunks, 2, half, cw), BF),
        pltpu.VMEM((tokens, width), F32),
        pltpu.VMEM((n_dp, rows, width), BF),
        pltpu.VMEM((n_dp, rows, width), BF),
        pltpu.VMEM((rows, width), BF),
        dma((5,)), dma((chunks,)), dma((slots,)),
        dma((max(n_dp - 1, 1),)), dma((max(n_dp - 1, 1),)), dma, dma,
        dma((chunks,)), dma((chunks,)),
        dma((peers, chunks)), dma((peers, chunks)),
        dma((chunks,)), dma((chunks,)),
        dma((n_dp,)), dma((n_dp,)),
        dma((n_t - 1,)), dma((n_t - 1,)), dma,
    ]
    return pl.pallas_call(
        functools.partial(kernel, sizes),
        out_shape=jax.ShapeDtypeStruct(layer_in.shape, BF),
        in_specs=[pl.BlockSpec(memory_space=pl.ANY)] * 7,
        out_specs=pl.BlockSpec(memory_space=pl.ANY),
        scratch_shapes=scratch,
        compiler_params=pltpu.CompilerParams(
            collective_id=0, has_side_effects=True, vmem_limit_bytes=67000000),
    )(layer_in, ln_gain, ln_bias, w_up, b_up, w_down, b_down)


def solution(mesh):
    counts = [mesh.shape[name] for name in ("section", "dp", "tensor")]
    return jax.shard_map(
        functools.partial(shards, *counts),
        mesh=mesh,
        in_specs=(
            P("section", "dp", None),
            P("section", None),
            P("section", None),
            P("section", "tensor", "dp"),
            P("section", "dp"),
            P("section", "dp", "tensor"),
            P("section", "tensor"),
        ),
        out_specs=P("section", "dp", None),
        check_vma=False,
    )
```

time: 128 us -> 37.2 us (0.29)
  waiting for transfers between devices: 50.8 us -> 0 us
  Pallas kernels: 0 us -> 35.4 us
  matrix products: 28.8 us -> 0 us
  blocking collectives: 27.3 us -> 0 us
  between operations: 13.4 us -> 0.01 us
  other arithmetic: 4.26 us -> 0 us
  starting transfers between devices: 1.51 us -> 0 us
    reduce_scatter x2 -> x0, waiting for transfers between devices: 46.5 us -> none  [the longest x1 26.3 us: shards(): lax.psum_scatter(partial_up, 'tensor', scatter_dimension=0, tiled=True)]
    pallas_call x0 -> x1, Pallas kernels: none -> 35.4 us  [shards(): pl.pallas_call(functools.partial(kernel, sizes), out_shape=jax.ShapeDtype...]
    dot_general x2 -> x0, matrix products: 28.8 us -> none  [the longest x1 14.6 us: shards(): jnp.dot(lax.all_gather(normed, 'dp', axis=0, tiled=True), up_local, prefe...]
    all_gather x3 -> x0, blocking collectives: 27.3 us -> none  [the longest x1 15.1 us: shards(): lax.all_gather(normed, 'dp', axis=0, tiled=True)]
    ppermute x1 -> x0, waiting for transfers between devices: 4.28 us -> none  [shifted(): return lax.ppermute(value, axis, pairs)]
    reduce_sum x2 -> x0, other arithmetic: 2.25 us -> none  [the longest x1 1.15 us: shards(): spread = jnp.mean(jnp.square(values - center), axis=1, keepdims=True)]
    convert_element_type x4 -> x0, other arithmetic: 2 us -> none  [the longest x1 1.05 us: shards(): jax.nn.gelu(share + b_up[0], approximate=True).astype(jnp.bfloat16)]
    ppermute x1 -> x0, starting transfers between devices: 1.46 us -> none  [shifted(): return lax.ppermute(value, axis, pairs)]
  transfers between devices with their start and end apart: 3 -> 0, of which waited for: 3 -> 0; matrix products, arithmetic and copies ran while one was open for 0% -> 0% of each run, Pallas kernels for 0% -> 0%
where the time goes in v1:
time: 37.2 us; the launch traced here: 37 us
  Pallas kernels  35.4 us (95%)
  local copies, waits for them, and re-layouts  1.57 us (4%)
    pallas_call x1, Pallas kernels, shards(): pl.pallas_call(functools.partial(kernel, sizes), out_shape=jax.ShapeDtype...  35.4 us
    unnamed x1, local copies, waits for them, and re-layouts  1.57 us

profile of v1, /device:TPU:0, one launch (start us, length us, event | category | flops | bytes accessed | tf_op | source)
XLA Modules:
  0.0 37.0 jit_solution(4187247259163859081)
XLA Ops:
  0.0 35.4 %shard_map.73 = bf16[1,8,8192]{2,1,0:T(8,128)(2,1)} custom-call(bf16[1,8,8192]{2,1,0:T(8,128)(2,1)} %x_hbm.1, f32[1,8192]{1,0:T(1,128)} %gain_hbm.1, f32[1,8192]{1,0:T(1,128)} %shift_hbm.1, bf16[1,2048,8192]{2,1,0:T(8,128)(2,1)} %up_hbm.1, f32[1,8192]{1,0:T(1,128)} %bup_hbm.1, bf16[1,8192,2048]{2,1,0:T(8,128)(2,1)} %down_hbm.1, f32[1,2048]{1,0:T(1,128)} %bdown_hbm.1), custom_call_target="tpu_custom_call" | custom-call | tf_op jit(solution)/shard_map/pallas_call | solution.py:269
  35.4 1.6 %copy.9 = bf16[1,8,8192]{2,1,0:T(8,128)(2,1)} copy(bf16[1,8,8192]{2,1,0:T(8,128)(2,1)} %shard_map.73) | data formatting | bytes 262144

commit v2 on v1

--- a/solution.py
+++ b/solution.py
@@ -10,9 +10,9 @@
 MESH = pl.DeviceIdType.MESH
 BF = jnp.bfloat16
 F32 = jnp.float32
-LAG_ACROSS = 3
-LAG_GELU = 9
-LAG_DOWN = 12
+LAG_ACROSS = 2
+LAG_GELU = 6
+LAG_DOWN = 8
 
 
 def gelu(v):
@@ -22,21 +22,21 @@
 def kernel(
     sizes,
     x_hbm, gain_hbm, shift_hbm, up_hbm, bup_hbm, down_hbm, bdown_hbm,
-    out_hbm,
+    out_ref,
     x_v, gain_v, shift_v, bup_v, bdown_v,
-    up_v, down_v,
+    up_v, down_v, col_v,
     norm_s, norm_r, lhs_v,
     resid_s, resid_r,
     pair_s, pair_r, keep_v,
     across_s, across_r,
     hid_v, acc_v,
     part_s, part_r, fin_v,
-    in_sem, up_sem, down_sem,
+    in_sem, up_sem, down_sem, col_sem,
     norm_ss, norm_rs, resid_ss, resid_rs,
     pair_ss, pair_rs, across_ss, across_rs, hid_ss, hid_rs,
     part_ss, part_rs, fin_ss, fin_rs, own_sem,
 ):
-    n_sec, n_dp, n_t, chunks, slots, rows, width, cw = sizes
+    n_sec, n_dp, n_t, chunks, lines, blocks, rows, width, cw = sizes
     outer = n_t // 2
     half = rows * n_dp // 2
     s = lax.axis_index("section")
@@ -53,8 +53,7 @@
         pl.semaphore_signal(barrier, inc=1, device_id=(s, lax.rem(d + k, n_dp), t), device_id_type=MESH)
     for k in range(1, n_t):
         pl.semaphore_signal(barrier, inc=1, device_id=(s, d, lax.rem(t + k, n_t)), device_id_type=MESH)
-    for k in range(n_dp):
-        pl.semaphore_signal(barrier, inc=1, device_id=(prv, lax.rem(d + k, n_dp), t), device_id_type=MESH)
+    pl.semaphore_signal(barrier, inc=1, device_id=(prv, d, t), device_id_type=MESH)
 
     small = [
         pltpu.make_async_copy(x_hbm.at[0], x_v, in_sem.at[0]),
@@ -71,9 +70,16 @@
         return pltpu.make_async_copy(up_hbm.at[0, :, columns], up_v.at[c], up_sem.at[c])
 
     def down_copy(c):
-        lines = pl.ds(pl.multiple_of(c * cw, cw), cw)
-        slot = lax.rem(c, slots)
-        return pltpu.make_async_copy(down_hbm.at[0, lines, :], down_v.at[slot], down_sem.at[slot])
+        part = pl.ds(pl.multiple_of(c * cw, cw), cw)
+        return pltpu.make_async_copy(down_hbm.at[0, part, :], down_v.at[c], down_sem.at[c])
+
+    reuse = blocks == chunks - lines and blocks * cw == width
+    col_place = up_v if reuse else col_v
+
+    def col_copy(n):
+        part = pl.ds(lines * cw, (chunks - lines) * cw)
+        columns = pl.ds(pl.multiple_of(n * cw, cw), cw)
+        return pltpu.make_async_copy(down_hbm.at[0, part, columns], col_place.at[n], col_sem.at[n])
 
     def run(count, body):
         def step(i, carry):
@@ -82,7 +88,9 @@
         lax.fori_loop(0, count, step, 0)
 
     run(chunks, lambda c: up_copy(c).start())
-    run(slots, lambda c: down_copy(c).start())
+    run(lines, lambda c: down_copy(c).start())
+    if not reuse:
+        run(blocks, lambda n: col_copy(n).start())
 
     for copy in small[:4]:
         copy.wait()
@@ -93,7 +101,7 @@
     normed = (own - center) * lax.rsqrt(spread + 1e-05) * gain_v[...] + shift_v[...]
     norm_s[...] = normed.astype(BF)
     resid_s[...] = own + bdown_v[...]
-    pl.semaphore_wait(barrier, 2 * n_dp + n_t - 2)
+    pl.semaphore_wait(barrier, n_dp + n_t - 1)
 
     def norm_copy(k):
         return pltpu.make_async_remote_copy(
@@ -136,6 +144,10 @@
         pair_s[c] = jnp.where(first, pre[half:], pre[:half]).astype(BF)
         pair_copy(c).start()
         keep_v[c] = jnp.where(first, pre[:half], pre[half:])
+        if reuse:
+            @pl.when(c < blocks)
+            def _():
+                col_copy(c).start()
 
     def across_stage(c):
         pair_copy(c).wait_recv()
@@ -154,56 +166,65 @@
         hid_v[c, core] = gelu(total).astype(BF)
         hid_copy(c).start()
 
+    def hid_wait(c):
+        pltpu.make_async_remote_copy(
+            hid_v.at[c, 1 - core], hid_v.at[c, 1 - core], hid_ss.at[c], hid_rs.at[c],
+            device_id=(s, d, partner), device_id_type=MESH).wait_recv()
+
     def down_stage(c):
-        other = pltpu.make_async_remote_copy(
-            hid_v.at[c, 1 - core], hid_v.at[c, 1 - core], hid_ss.at[c], hid_rs.at[c],
-            device_id=(s, d, partner), device_id_type=MESH)
-        other.wait_recv()
+        hid_wait(c)
         down_copy(c).wait()
         acc_v[...] += jnp.dot(
-            hid_v[c].reshape(2 * half, cw), down_v[lax.rem(c, slots)], preferred_element_type=F32)
-        if slots < chunks:
-            @pl.when(c + slots < chunks)
-            def _():
-                down_copy(c + slots).start()
-
-    stages = ((0, up_stage), (LAG_ACROSS, across_stage), (LAG_GELU, gelu_stage), (LAG_DOWN, down_stage))
+            hid_v[c].reshape(2 * half, cw), down_v[c], preferred_element_type=F32)
+
+    stages = (
+        (0, chunks, up_stage),
+        (LAG_ACROSS, chunks, across_stage),
+        (LAG_GELU, chunks, gelu_stage),
+        (LAG_DOWN, lines, down_stage),
+    )
 
     def tick(i):
-        for lag, stage in stages:
-            @pl.when((i >= lag) & (i < lag + chunks))
+        for lag, count, stage in stages:
+            @pl.when((i >= lag) & (i < lag + count))
             def _():
                 stage(i - lag)
 
-    run(chunks + LAG_DOWN, tick)
-
-    part_s[...] = acc_v[...].reshape(n_dp, rows, width).astype(BF)
-
-    def part_copy(k):
+    run(max(chunks + LAG_GELU, lines + LAG_DOWN), tick)
+    for c in range(lines, chunks):
+        hid_wait(c)
+
+    def part_copy(n, k):
         target = lax.rem(d + k, n_dp)
         return pltpu.make_async_remote_copy(
-            part_s.at[target], part_r.at[k], part_ss.at[k], part_rs.at[k],
+            part_s.at[n, target], part_r.at[n, k], part_ss.at[n, k], part_rs.at[n, k],
             device_id=(nxt, target, t), device_id_type=MESH)
 
-    for k in range(n_dp):
-        part_copy(k).start()
+    def place(n):
+        return out_ref.at[0, :, pl.ds(pl.multiple_of(offset + n * cw, cw), cw)]
+
+    def fin_copy(n, k):
+        return pltpu.make_async_remote_copy(
+            fin_v.at[n], place(n), fin_ss.at[n, k - 1], fin_rs.at[n, k - 1],
+            device_id=(s, d, lax.rem(t + k, n_t)), device_id_type=MESH)
+
+    for n in range(blocks):
+        col_copy(n).wait()
+        last = jnp.concatenate([hid_v[c].reshape(2 * half, cw) for c in range(lines, chunks)], axis=1)
+        part = acc_v[:, n * cw:(n + 1) * cw] + jnp.dot(last, col_place[n], preferred_element_type=F32)
+        part_s[n] = part.reshape(n_dp, rows, cw).astype(BF)
+        for k in range(n_dp):
+            part_copy(n, k).start()
     resid_copy.wait_recv()
-    total = resid_r[...]
-    for k in range(n_dp):
-        part_copy(k).wait_recv()
-        total = total + part_r[k].astype(F32)
-    fin_v[...] = total.astype(BF)
-
-    def fin_copy(k):
-        place = out_hbm.at[0, :, pl.ds(offset, width)]
-        return pltpu.make_async_remote_copy(
-            fin_v, place, fin_ss.at[k - 1], fin_rs.at[k - 1],
-            device_id=(s, d, lax.rem(t + k, n_t)), device_id_type=MESH)
-
-    for k in range(1, n_t):
-        fin_copy(k).start()
-    fin_own = pltpu.make_async_copy(fin_v, out_hbm.at[0, :, pl.ds(offset, width)], own_sem)
-    fin_own.start()
+    for n in range(blocks):
+        total = resid_r[:, n * cw:(n + 1) * cw]
+        for k in range(n_dp):
+            part_copy(n, k).wait_recv()
+            total = total + part_r[n, k].astype(F32)
+        fin_v[n] = total.astype(BF)
+        for k in range(1, n_t):
+            fin_copy(n, k).start()
+        place(n)[...] = total.astype(BF)
 
     for k in range(1, n_dp):
         norm_copy(k).wait_send()
@@ -216,24 +237,27 @@
         hid_copy(c).wait_send()
 
     run(chunks, drain)
-    for k in range(n_dp):
-        part_copy(k).wait_send()
-    fin_own.wait()
-    for k in range(1, n_t):
-        fin_copy(k).wait()
+    for n in range(blocks):
+        for k in range(n_dp):
+            part_copy(n, k).wait_send()
+    for n in range(blocks):
+        for k in range(1, n_t):
+            fin_copy(n, k).wait()
 
 
 def shards(n_sec, n_dp, n_t, layer_in, ln_gain, ln_bias, w_up, b_up, w_down, b_down):
     rows = layer_in.shape[1]
     width, units = w_up.shape[1], w_up.shape[2]
-    cw = 512 if units % 512 == 0 else units
+    cw = 1024 if units % 1024 == 0 else units
     chunks = units // cw
-    slots = min(chunks, 12)
+    blocks = width // cw
+    lines = max(chunks - blocks, 0)
+    reuse = chunks - lines == blocks
     tokens = rows * n_dp
     half = tokens // 2
     outer = n_t // 2
     peers = max(outer - 1, 1)
-    sizes = (n_sec, n_dp, n_t, chunks, slots, rows, width, cw)
+    sizes = (n_sec, n_dp, n_t, chunks, lines, blocks, rows, width, cw)
     dma = pltpu.SemaphoreType.DMA
     scratch = [
         pltpu.VMEM((rows, layer_in.shape[2]), BF),
@@ -242,7 +266,8 @@
         pltpu.VMEM((1, units), F32),
         pltpu.VMEM((1, width), F32),
         pltpu.VMEM((chunks, width, cw), BF),
-        pltpu.VMEM((slots, cw, width), BF),
+        pltpu.VMEM((max(lines, 1), cw, width), BF),
+        pltpu.VMEM((1, 16, 128) if reuse else (blocks, (chunks - lines) * cw, cw), BF),
         pltpu.VMEM((rows, width), BF),
         pltpu.VMEM((n_dp, rows, width), BF),
         pltpu.VMEM((tokens, width), BF),
@@ -255,25 +280,25 @@
         pltpu.VMEM((peers, chunks, half, cw), BF),
         pltpu.VMEM((chunks, 2, half, cw), BF),
         pltpu.VMEM((tokens, width), F32),
-        pltpu.VMEM((n_dp, rows, width), BF),
-        pltpu.VMEM((n_dp, rows, width), BF),
-        pltpu.VMEM((rows, width), BF),
-        dma((5,)), dma((chunks,)), dma((slots,)),
+        pltpu.VMEM((blocks, n_dp, rows, cw), BF),
+        pltpu.VMEM((blocks, n_dp, rows, cw), BF),
+        pltpu.VMEM((blocks, rows, cw), BF),
+        dma((5,)), dma((chunks,)), dma((max(lines, 1),)), dma((blocks,)),
         dma((max(n_dp - 1, 1),)), dma((max(n_dp - 1, 1),)), dma, dma,
         dma((chunks,)), dma((chunks,)),
         dma((peers, chunks)), dma((peers, chunks)),
         dma((chunks,)), dma((chunks,)),
-        dma((n_dp,)), dma((n_dp,)),
-        dma((n_t - 1,)), dma((n_t - 1,)), dma,
+        dma((blocks, n_dp)), dma((blocks, n_dp)),
+        dma((blocks, n_t - 1)), dma((blocks, n_t - 1)), dma,
     ]
     return pl.pallas_call(
         functools.partial(kernel, sizes),
-        out_shape=jax.ShapeDtypeStruct(layer_in.shape, BF),
+        out_shape=pltpu.VMEM(layer_in.shape, BF),
         in_specs=[pl.BlockSpec(memory_space=pl.ANY)] * 7,
-        out_specs=pl.BlockSpec(memory_space=pl.ANY),
+        out_specs=pl.BlockSpec(memory_space=pltpu.VMEM),
         scratch_shapes=scratch,
         compiler_params=pltpu.CompilerParams(
-            collective_id=0, has_side_effects=True, vmem_limit_bytes=67000000),
+            collective_id=0, has_side_effects=True, vmem_limit_bytes=63 * 1024 * 1024),
     )(layer_in, ln_gain, ln_bias, w_up, b_up, w_down, b_down)
 
 

time: 37.2 us -> 34.2 us (0.919)
  Pallas kernels: 35.4 us -> 33.4 us
  local copies, waits for them, and re-layouts: 1.57 us -> 0.66 us
    pallas_call x1, Pallas kernels: 35.4 us -> 33.4 us  [shards(): pl.pallas_call(functools.partial(kernel, sizes), out_shape=pltpu.VMEM(lay...]
    unnamed x1, local copies, waits for them, and re-layouts: 1.57 us -> 0.66 us
where the time goes in v2:
time: 34.2 us; the launch traced here: 34 us
  Pallas kernels  33.4 us (98%)
  local copies, waits for them, and re-layouts  0.66 us (2%)
    pallas_call x1, Pallas kernels, shards(): pl.pallas_call(functools.partial(kernel, sizes), out_shape=pltpu.VMEM(lay...  33.4 us

profile of v2, /device:TPU:0, one launch (start us, length us, event | category | flops | bytes accessed | tf_op | source)
XLA Modules:
  0.0 34.0 jit_solution(17861239684561468296)
XLA Ops:
  0.0 33.4 %shard_map.73 = bf16[1,8,8192]{2,1,0:T(8,128)(2,1)S(1)} custom-call(bf16[1,8,8192]{2,1,0:T(8,128)(2,1)} %x_hbm.1, f32[1,8192]{1,0:T(1,128)} %gain_hbm.1, f32[1,8192]{1,0:T(1,128)} %shift_hbm.1, bf16[1,2048,8192]{2,1,0:T(8,128)(2,1)} %up_hbm.1, f32[1,8192]{1,0:T(1,128)} %bup_hbm.1, bf16[1,8192,2048]{2,1,0:T(8,128)(2,1)} %down_hbm.1, f32[1,2048]{1,0:T(1,128)} %bdown_hbm.1), custom_call_target="tpu_custom_call" | custom-call | tf_op jit(solution)/shard_map/pallas_call | solution.py:294
  33.4 0.7 %copy.9 = bf16[1,8,8192]{2,1,0:T(8,128)(2,1)} copy(bf16[1,8,8192]{2,1,0:T(8,128)(2,1)S(1)} %shard_map.73) | data formatting | bytes 262144
